TPU v7x, 256 devices: a whole 4x4x8 slice. The times are simulated.
256 devices in a mesh: tm: 32 (over x, z), tensor: 8 (over y, core).
Axes of the slice: x: 4, y: 4, z: 8, core: 2. Of those that a mesh axis runs over, the one named last changes fastest.
Arguments:
- latents: float32 [32, 640, 64], P('tm', 'tensor'), may hold values from -6 to 6
- residual: bfloat16 [32, 640, 5120], P('tm'), may hold values from -6 to 6
- timesteps: int32 [32], P('tm'), may hold values from 0 to 999
- step_sizes: float32 [32], P('tm'), may hold values from 0.015 to 0.06
- embed_weight: bfloat16 [64, 5120], replicated
- mod_weight: bfloat16 [3, 256, 5120], P(None, None, 'tensor'), may hold values from -0.75 to 0.75
- up_weight: bfloat16 [5120, 7168], P('tm', 'tensor'), may hold values from -0.078125 to 0.078125
- down_weight: bfloat16 [7168, 5120], P('tensor', 'tm'), may hold values from -0.0625 to 0.0625
- head_weight: bfloat16 [5120, 64], replicated, may hold values from -0.078125 to 0.078125
Outputs:
- drift: float32 [32, 640, 64], P('tm', 'tensor')
- new_latents: float32 [32, 640, 64], P('tm', 'tensor')
All inputs are finite; a program needn't handle non-finite values.
Results may differ from a plain program's by a relative error of at most 0.0085.
Values may be sent and summed in bfloat16 or wider, within the bound.
No kernel may reach another device: no remote copies, remote signals or barrier semaphores. Data moves between devices by JAX's collectives and lax.ppermute only.
A program may use at most 128 MiB of HBM per device.

v0:
```python
import math
import jax
import jax.numpy as jnp
from jax import lax
from jax.sharding import PartitionSpec as P


def prefix(part, axis, combine, identity):
    place = lax.axis_index(axis)
    gathered = lax.all_gather(part, axis)
    state = jnp.zeros_like(part) + jnp.asarray(identity, part.dtype)

    def one(hop, state):
        return combine(state, lax.dynamic_index_in_dim(gathered, hop, 0, False))

    return lax.fori_loop(0, place, one, state)


def normalize(values):
    centre = values - jnp.mean(values, axis=-1, keepdims=True)
    spread = jnp.mean(centre * centre, axis=-1, keepdims=True)
    return centre * lax.rsqrt(spread + 1e-06)


def time_features(stamps, width):
    half = width // 2
    freqs = jnp.exp(-math.log(10000.0) * jnp.arange(half, dtype=jnp.float32) / half)
    angles = stamps.astype(jnp.float32)[:, None] * freqs[None, :]
    return jnp.concatenate([jnp.cos(angles), jnp.sin(angles)], axis=-1)


def add_terms(earlier, later):
    return earlier + later


def local(
    latents,
    residual,
    timesteps,
    step_sizes,
    embed_weight,
    mod_weight,
    up_weight,
    down_weight,
    head_weight,
):
    feature = jax.nn.silu(time_features(timesteps, mod_weight.shape[1])).astype(jnp.bfloat16)[0]
    piece_mod = jnp.einsum("f,kfd->kd", feature, mod_weight, preferred_element_type=jnp.float32)
    modulation = lax.all_gather(piece_mod, "tensor", axis=1, tiled=True)
    latent = latents[0]
    stream = residual[0]
    latent_bf = latent.astype(jnp.bfloat16)
    own_rows = latent.shape[0]
    row_start = lax.axis_index("tensor") * own_rows
    own_stream = lax.dynamic_slice_in_dim(stream, row_start, own_rows, 0)
    hidden = own_stream.astype(jnp.float32) + jnp.dot(
        latent_bf, embed_weight, preferred_element_type=jnp.float32
    )
    local_normed = (normalize(hidden) * (1.0 + modulation[1]) + modulation[0]).astype(jnp.bfloat16)
    normed = lax.all_gather(local_normed, "tensor", axis=0, tiled=True)
    preact = jnp.dot(
        normed,
        lax.all_gather(up_weight, "tm", axis=0, tiled=True),
        preferred_element_type=jnp.float32,
    )
    activated = jax.nn.gelu(preact, approximate=True).astype(jnp.bfloat16)
    partial_sums = jnp.dot(
        activated,
        lax.all_gather(down_weight, "tm", axis=1, tiled=True),
        preferred_element_type=jnp.float32,
    )
    mixed = lax.psum_scatter(
        partial_sums.astype(jnp.bfloat16), "tensor", scatter_dimension=0, tiled=True
    ).astype(jnp.float32)
    updated = hidden + modulation[2] * mixed
    drift = jnp.dot(
        normalize(updated).astype(jnp.bfloat16), head_weight, preferred_element_type=jnp.float32
    )
    position = lax.axis_index("tm")
    first = (position == 0).astype(jnp.float32)
    term = first * latent - step_sizes[0] * drift
    earlier = prefix(term, "tm", add_terms, jnp.zeros_like(term))
    new_latent = earlier + term
    return (drift[None], new_latent[None])


def solution(mesh):
    in_specs = (
        P("tm", "tensor", None),
        P("tm", None, None),
        P("tm"),
        P("tm"),
        P(),
        P(None, None, "tensor"),
        P("tm", "tensor"),
        P("tensor", "tm"),
        P(),
    )
    out_specs = (P("tm", "tensor", None), P("tm", "tensor", None))
    return jax.shard_map(local, mesh=mesh, in_specs=in_specs, out_specs=out_specs, check_vma=False)
```

profile of v0, /device:TPU:6, one launch (start us, length us, event | category | flops | bytes accessed | tf_op | source)
XLA Modules:
  0.0 398.8 jit_solution(11767064728763271483)
XLA Ops:
  7.2 1.9 fusion.28
  9.2 0.3 multiply_reduce_fusion.1
  10.3 0.2 fusion.29
  10.5 13.3 %all_gather.18 = f32[3,5120]{1,0:T(4,128)S(1)} all-gather(f32[3,640]{1,0:T(4,128)S(1)} %bitcast.46), channel_id=1, replica_groups=mesh['tm'=32,'tensor'=8] {'tensor'}, dimensions={1}, use_global_device_ids=true | all-gather | bytes 69120 | tf_op jit(solution)/shard_map/all_gather | solution.py:49
  23.9 1.3 add_convert_fusion
  25.2 0.7 all-gather.8.cloned.1.call-update
  26.0 0.7 all-gather.10.cloned.1.call-update
  26.7 45.4 %all-gather.6.cloned.1.call-done = bf16[640,5120]{1,0:T(8,128)(2,1)} async-done(((bf16[80,5120]{1,0:T(8,128)(2,1)}), bf16[640,5120]{1,0:T(8,128)(2,1)}) %all-gather.6.cloned.1.call-update) | async-done | bytes 6553616 | tf_op jit(solution)/shard_map/all_gather | solution.py:60
  72.2 103.0 %all-gather.8.cloned.1.call-done = bf16[5120,896]{1,0:T(8,128)(2,1)} async-done(((bf16[160,896]{1,0:T(8,128)(2,1)}), bf16[5120,896]{1,0:T(8,128)(2,1)}) %all-gather.8.cloned.1.call-update) | async-done | bytes 9175056 | tf_op jit(solution)/shard_map/all_gather | solution.py:63
  175.2 12.7 %fusion.30 = f32[640,896]{1,0:T(8,128)} fusion(bf16[640,5120]{1,0:T(8,128)(2,1)} %all-gather.6.cloned.1.call-done, bf16[5120,896]{1,0:T(8,128)(2,1)} %all-gather.8.cloned.1.call-done), kind=kOutput, calls=%fused_computation.50 | convolution fusion | flops 5872025600 | bytes 18022400 | tf_op jit(solution)/shard_map/dot_general | solution.py:61
  187.9 89.2 %all-gather.10.cloned.1.call-done = bf16[896,5120]{0,1:T(8,128)(2,1)} async-done(((bf16[896,160]{0,1:T(8,128)(2,1)}), bf16[896,5120]{0,1:T(8,128)(2,1)}) %all-gather.10.cloned.1.call-update) | async-done | bytes 9175056 | tf_op jit(solution)/shard_map/all_gather | solution.py:69
  277.1 12.2 %convolution_convert_fusion = bf16[640,5120]{1,0:T(8,128)(2,1)} fusion(bf16[896,5120]{0,1:T(8,128)(2,1)} %all-gather.10.cloned.1.call-done, f32[640,896]{1,0:T(8,128)} %fusion.30), kind=kOutput, calls=%fused_computation.2 | convolution fusion | flops 5880463360 | bytes 18022400 | tf_op jit(solution)/shard_map/dot_general | solution.py:67
  289.9 44.7 %reduce-scatter.2.cloned.1.call-done = bf16[80,5120]{1,0:T(8,128)(2,1)} async-done(((bf16[640,5120]{1,0:T(8,128)(2,1)}), bf16[80,5120]{1,0:T(8,128)(2,1)}) %reduce-scatter.2.cloned.1.call-update) | async-done | bytes 819216 | tf_op jit(solution)/shard_map/reduce_scatter | solution.py:72
  334.6 1.5 fusion.16
  336.2 0.5 multiply_reduce_fusion
  336.7 0.6 copy-done.2
  337.3 0.6 fusion.13
  337.9 50.2 %all-gather.1 = f32[32,80,64]{1,2,0:T(8,128)S(1)} all-gather(f32[1,80,64]{1,2,0:T(8,128)S(1)} %fusion.19), channel_id=2, replica_groups=mesh['tm'=32,'tensor'=8] {'tm'}, dimensions={0}, use_global_device_ids=true | all-gather | bytes 675840 | tf_op jit(solution)/shard_map/all_gather | solution.py:10
  388.1 3.4 while.10
  388.2 0.1 copy.20
  388.3 0.1 copy.20
  388.4 0.1 copy.20
  388.6 0.1 copy.20
  388.7 0.1 copy.20
  388.9 0.1 copy.20
  389.0 0.1 copy.20
  389.2 0.1 copy.20
  389.3 0.1 copy.20
  389.4 0.1 copy.20
  389.6 0.1 copy.20
  389.7 0.1 copy.20
  391.6 0.6 add_bitcast_fusion
  (87 shorter events, 1.8 us)
Async XLA Ops:
  7.2 3.1 copy-start
  7.2 65.0 %all-gather.6.cloned.1.call-start = ((), (), s32[]{:S(2)}) async-start(), calls=%async_computation.1 | async-start | bytes 7372800 | tf_op jit(solution)/shard_map/all_gather | solution.py:60
  25.2 150.0 %all-gather.8.cloned.1.call-start = ((), (), s32[]{:S(2)}) async-start(), calls=%async_computation.2 | async-start | bytes 9461760 | tf_op jit(solution)/shard_map/all_gather | solution.py:63
  26.0 251.1 %all-gather.10.cloned.1.call-start = ((), (), s32[]{:S(2)}) async-start(), calls=%async_computation.3 | async-start | bytes 9461760 | tf_op jit(solution)/shard_map/all_gather | solution.py:69
  26.7 307.9 %reduce-scatter.2.cloned.1.call-start = ((), (), s32[]{:S(2)}) async-start(), calls=%async_computation.4 | async-start | bytes 7372800 | tf_op jit(solution)/shard_map/reduce_scatter | solution.py:72
  334.6 1.6 copy-start.1
  336.2 1.1 copy-start.2
  336.7 1.2 copy-start.3
  337.9 54.4 %copy-start.4 = (f32[80,64]{0,1:T(8,128)}, f32[80,64]{0,1:T(8,128)S(1)}, u32[]{:S(2)}) copy-start(f32[80,64]{0,1:T(8,128)S(1)} %fusion.13) | copy-start | bytes 61444
Sparse Core Ops, SparseCore 0:
  25.3 46.7 all-gather.5
  74.7 100.4 all-gather.7
  177.8 99.2 all-gather.9
  289.4 45.1 reduce-scatter.1
where the time goes:
time: 399 us
  waiting for transfers between devices  284 us (71%)
  blocking collectives  63.5 us (16%)
  matrix products  27.6 us (7%)
  between operations  15.2 us (4%)
  other arithmetic  4.66 us (1%)
    all_gather x1, waiting for transfers between devices, local(): lax.all_gather(up_weight, 'tm', axis=0, tiled=True)  103 us
    all_gather x1, waiting for transfers between devices, local(): lax.all_gather(down_weight, 'tm', axis=1, tiled=True)  89.2 us
    all_gather x1, blocking collectives, prefix(): gathered = lax.all_gather(part, axis)  50.2 us
    all_gather x1, waiting for transfers between devices, local(): normed = lax.all_gather(local_normed, 'tensor', axis=0, tiled=True)  45.4 us
    reduce_scatter x1, waiting for transfers between devices, local(): lax.psum_scatter(partial_sums.astype(jnp.bfloat16), 'tensor', scatter_dim...  44.7 us
    all_gather x1, blocking collectives, local(): modulation = lax.all_gather(piece_mod, 'tensor', axis=1, tiled=True)  13.3 us
    dot_general x1, matrix products, local(): jnp.dot(normed, lax.all_gather(up_weight, 'tm', axis=0, tiled=True), pref...  12.7 us
    dot_general x1, matrix products, local(): jnp.dot(activated, lax.all_gather(down_weight, 'tm', axis=1, tiled=True),...  12.2 us
  transfers between devices with their start and end apart: 4, of which 4 were waited for; matrix products, arithmetic and copies ran while one was open for 3% of the time, Pallas kernels for 0%

commit v1 on v0

--- a/solution.py
+++ b/solution.py
@@ -57,7 +57,9 @@
         latent_bf, embed_weight, preferred_element_type=jnp.float32
     )
     local_normed = (normalize(hidden) * (1.0 + modulation[1]) + modulation[0]).astype(jnp.bfloat16)
-    normed = lax.all_gather(local_normed, "tensor", axis=0, tiled=True)
+    normed = jnp.concatenate(
+        lax.all_to_all(jnp.stack([local_normed] * lax.axis_size("tensor")), "tensor", 0, 0), axis=0
+    )
     preact = jnp.dot(
         normed,
         lax.all_gather(up_weight, "tm", axis=0, tiled=True),

time: 399 us -> 338 us (0.85)
  waiting for transfers between devices: 284 us -> 143 us
  blocking collectives: 63.5 us -> 143 us
    all_gather x1, waiting for transfers between devices: 103 us -> 8.06 us  [local(): lax.all_gather(up_weight, 'tm', axis=0, tiled=True)]
    all_to_all x0 -> x1, blocking collectives: none -> 79.7 us  [local(): lax.all_to_all(jnp.stack([local_normed] * lax.axis_size('tensor')), 'tens...]
    all_gather x1 -> x0, waiting for transfers between devices: 45.4 us -> none  [local(): normed = lax.all_gather(local_normed, 'tensor', axis=0, tiled=True)]
  transfers between devices with their start and end apart: 4 -> 3, of which waited for: 4 -> 3; matrix products, arithmetic and copies ran while one was open for 3% -> 5% of each run, Pallas kernels for 0% -> 0%
where the time goes in v1:
time: 338 us
  waiting for transfers between devices  143 us (42%)
  blocking collectives  143 us (42%)
  matrix products  27.4 us (8%)
  between operations  15.2 us (4%)
  other arithmetic  3.7 us (1%)
  local copies, waits for them, and re-layouts  3.6 us (1%)
    all_gather x1, waiting for transfers between devices, local(): lax.all_gather(down_weight, 'tm', axis=1, tiled=True)  89.2 us
    all_to_all x1, blocking collectives, local(): lax.all_to_all(jnp.stack([local_normed] * lax.axis_size('tensor')), 'tens...  79.7 us
    all_gather x1, blocking collectives, prefix(): gathered = lax.all_gather(part, axis)  50.2 us
    reduce_scatter x1, waiting for transfers between devices, local(): lax.psum_scatter(partial_sums.astype(jnp.bfloat16), 'tensor', scatter_dim...  44.7 us
    all_gather x1, blocking collectives, local(): modulation = lax.all_gather(piece_mod, 'tensor', axis=1, tiled=True)  13.3 us
    dot_general x1, matrix products, local(): jnp.dot(normed, lax.all_gather(up_weight, 'tm', axis=0, tiled=True), pref...  12.7 us
    dot_general x1, matrix products, local(): jnp.dot(activated, lax.all_gather(down_weight, 'tm', axis=1, tiled=True),...  12.3 us
    all_gather x1, waiting for transfers between devices, local(): lax.all_gather(up_weight, 'tm', axis=0, tiled=True)  8.06 us
  transfers between devices with their start and end apart: 3, of which 3 were waited for; matrix products, arithmetic and copies ran while one was open for 5% of the time, Pallas kernels for 0%

profile of v1, /device:TPU:6, one launch (start us, length us, event | category | flops | bytes accessed | tf_op | source)
XLA Modules:
  0.0 337.7 jit_solution(7281761011453096863)
XLA Ops:
  7.2 0.7 all-gather.5.cloned.1.call-update
  8.0 0.7 all-gather.7.cloned.1.call-update
  9.5 0.2 fusion.29
  9.7 13.3 %all_gather.15 = f32[3,5120]{1,0:T(4,128)S(1)} all-gather(f32[3,640]{1,0:T(4,128)S(1)} %bitcast.48), channel_id=1, replica_groups=mesh['tm'=32,'tensor'=8] {'tensor'}, dimensions={1}, use_global_device_ids=true | all-gather | bytes 69120 | tf_op jit(solution)/shard_map/all_gather | solution.py:49
  23.0 1.6 fusion.28
  24.7 0.3 multiply_reduce_fusion.1
  25.1 0.3 add_convert_fusion
  25.4 0.8 stack.2
  26.2 79.7 %all_to_all.5 = bf16[8,80,5120]{2,1,0:T(8,128)(2,1)} all-to-all(bf16[8,80,5120]{2,1,0:T(8,128)(2,1)S(1)} %stack.2), channel_id=1, replica_groups=mesh['tm'=32,'tensor'=8] {'tensor'}, dimensions={0} | all-to-all | bytes 13107200 | tf_op jit(solution)/shard_map/all_to_all | solution.py:61
  105.9 8.1 %all-gather.5.cloned.1.call-done = bf16[5120,896]{1,0:T(8,128)(2,1)} async-done(((bf16[160,896]{1,0:T(8,128)(2,1)}), bf16[5120,896]{1,0:T(8,128)(2,1)}) %all-gather.5.cloned.1.call-update) | async-done | bytes 9175056 | tf_op jit(solution)/shard_map/all_gather | solution.py:65
  114.0 12.7 %fusion.30 = f32[640,896]{1,0:T(8,128)} fusion(bf16[640,5120]{1,0:T(8,128)(2,1)} %bitcast.41, bf16[5120,896]{1,0:T(8,128)(2,1)} %all-gather.5.cloned.1.call-done), kind=kOutput, calls=%fused_computation.50 | convolution fusion | flops 5872025600 | bytes 18022400 | tf_op jit(solution)/shard_map/dot_general | solution.py:63
  126.7 89.2 %all-gather.7.cloned.1.call-done = bf16[896,5120]{0,1:T(8,128)(2,1)} async-done(((bf16[896,160]{0,1:T(8,128)(2,1)}), bf16[896,5120]{0,1:T(8,128)(2,1)}) %all-gather.7.cloned.1.call-update) | async-done | bytes 9175056 | tf_op jit(solution)/shard_map/all_gather | solution.py:71
  215.9 12.3 %convolution_convert_fusion = bf16[640,5120]{1,0:T(8,128)(2,1)} fusion(bf16[896,5120]{0,1:T(8,128)(2,1)} %all-gather.7.cloned.1.call-done, f32[640,896]{1,0:T(8,128)} %fusion.30), kind=kOutput, calls=%fused_computation.2 | convolution fusion | flops 5880463360 | bytes 18022400 | tf_op jit(solution)/shard_map/dot_general | solution.py:69
  228.8 44.7 %reduce-scatter.2.cloned.1.call-done = bf16[80,5120]{1,0:T(8,128)(2,1)} async-done(((bf16[640,5120]{1,0:T(8,128)(2,1)}), bf16[80,5120]{1,0:T(8,128)(2,1)}) %reduce-scatter.2.cloned.1.call-update) | async-done | bytes 819216 | tf_op jit(solution)/shard_map/reduce_scatter | solution.py:74
  273.6 1.5 fusion.16
  275.1 0.5 multiply_reduce_fusion
  275.6 0.6 copy-done.3
  276.2 0.6 fusion.13
  276.8 50.2 %all-gather.1 = f32[32,80,64]{1,2,0:T(8,128)S(1)} all-gather(f32[1,80,64]{1,2,0:T(8,128)S(1)} %fusion.19), channel_id=2, replica_groups=mesh['tm'=32,'tensor'=8] {'tm'}, dimensions={0}, use_global_device_ids=true | all-gather | bytes 675840 | tf_op jit(solution)/shard_map/all_gather | solution.py:10
  327.0 3.4 %while.10 = (s32[]{:T(128)}, f32[80,64]{1,0:T(8,128)S(1)}, s32[]{:T(128)}, f32[32,80,64]{1,2,0:T(8,128)S(1)}, s32[]{:T(128)}, /*index=5*/s32[]{:T(128)}, s32[]{:T(128)}) while((s32[]{:T(128)}, f32[80,64]{1,0:T(8,128)S(1)}, s32[]{:T(128)}, f32[32,80,64]{1,2,0:T(8,128)S(1)}, s32[]{:T(128)}, /*index=5*/s32[]{:T(128)}, s32[]{:T(128)}) %tuple.28), condition=%wide.region_6.7_spmd, body=%wide.region_5.6_spmd.sunk | while | flops 5125 | bytes 143475 | solution.py:16
  327.1 0.1 copy.20
  327.2 0.1 copy.20
  327.4 0.1 copy.20
  327.5 0.1 copy.20
  327.7 0.1 copy.20
  327.8 0.1 copy.20
  327.9 0.1 copy.20
  328.1 0.1 copy.20
  328.2 0.1 copy.20
  328.4 0.1 copy.20
  328.5 0.1 copy.20
  330.5 0.6 add_bitcast_fusion
  (88 shorter events, 1.9 us)
Async XLA Ops:
  7.2 2.3 copy-start
  7.2 15.8 %copy-start.4 = (f32[1,80,64]{1,2,0:T(8,128)S(1)}, f32[1,80,64]{1,2,0:T(8,128)}, u32[]{:S(2)}) copy-start(f32[1,80,64]{1,2,0:T(8,128)} %param.11) | copy-start | bytes 61444
  7.2 15.8 %copy-start.2 = (bf16[64,5120]{1,0:T(8,128)(2,1)S(1)}, bf16[64,5120]{1,0:T(8,128)(2,1)}, u32[]{:S(2)}) copy-start(bf16[64,5120]{1,0:T(8,128)(2,1)} %param.15) | copy-start | bytes 1966084
  7.2 106.8 %all-gather.5.cloned.1.call-start = ((), (), s32[]{:S(2)}) async-start(), calls=%async_computation.2 | async-start | bytes 9461760 | tf_op jit(solution)/shard_map/all_gather | solution.py:65
  7.9 207.9 %all-gather.7.cloned.1.call-start = ((), (), s32[]{:S(2)}) async-start(), calls=%async_computation.3 | async-start | bytes 9461760 | tf_op jit(solution)/shard_map/all_gather | solution.py:71
  8.7 264.9 %reduce-scatter.2.cloned.1.call-start = ((), (), s32[]{:S(2)}) async-start(), calls=%async_computation.4 | async-start | bytes 7372800 | tf_op jit(solution)/shard_map/reduce_scatter | solution.py:74
  273.6 1.6 copy-start.1
  275.1 1.1 copy-start.3
  276.8 54.4 %copy-start.5 = (f32[80,64]{0,1:T(8,128)}, f32[80,64]{0,1:T(8,128)S(1)}, u32[]{:S(2)}) copy-start(f32[80,64]{0,1:T(8,128)S(1)} %fusion.13) | copy-start | bytes 61444
Sparse Core Ops, SparseCore 0:
  10.6 103.3 all-gather.4
  116.5 99.2 all-gather.6
  228.3 45.2 reduce-scatter.1
